TPU v7x, 256 devices: a whole 4x4x8 slice. The times are simulated.
256 devices in a mesh: dp: 8 (over y, core), tensor: 32 (over x, z).
Axes of the slice: x: 4, y: 4, z: 8, core: 2. Of those that a mesh axis runs over, the one named last changes fastest.
Arguments:
- tokens: bfloat16 [2048, 8192], P('dp', 'tensor'), may hold values from -6 to 6
- pattern: int32 [256, 8], P('tensor'), may hold values from 0 to 63, as said below
- first_blocks: bfloat16 [256, 8, 128, 128], P('tensor'), may hold values from -0.1875 to 0.1875
- second_blocks: bfloat16 [256, 8, 128, 128], P('tensor'), may hold values from -0.1875 to 0.1875
- out_grad: bfloat16 [2048, 8192], P('dp', 'tensor'), may hold values from -0.75 to 0.75
Outputs:
- layer_out: bfloat16 [2048, 8192], P('dp', 'tensor')
- input_grad: bfloat16 [2048, 8192], P('dp', 'tensor')
- first_grad: bfloat16 [256, 8, 128, 128], P('tensor')
- second_grad: bfloat16 [256, 8, 128, 128], P('tensor')
Inputs may be any that keep to these rules, and one draw needn't show every extreme that they name: `pattern`: each hidden block row r lists 8 distinct feature blocks: r mod 64, the blocks that differ from it in bit 0, in bit 3 and in the highest bit, and 4 further ones drawn at random. Every feature block is listed by some row.
All inputs are finite; a program needn't handle non-finite values.
Results may differ from a plain program's by a relative error of at most 0.015.
Values may be sent and summed in bfloat16 or wider, within the bound.
A program may use at most 128 MiB of HBM per device.

v0:
```python
import jax
import jax.numpy as jnp
from jax import lax
from jax.sharding import PartitionSpec as P

gelu_scale = 0.7978845608028654
gelu_cube = 0.044715


def gelu_pair(value):
    inner = gelu_scale * (value + gelu_cube * value * value * value)
    tangent = jnp.tanh(inner)
    result = 0.5 * value * (1.0 + tangent)
    slope = 0.5 * (1.0 + tangent) + 0.5 * value * (1.0 - tangent * tangent) * gelu_scale * (
        1.0 + 3.0 * gelu_cube * value * value
    )
    return (result, slope)


def place_blocks(terms, pattern, count):
    targets = jnp.arange(count, dtype=jnp.int32)
    select = (pattern[:, :, None] == targets[None, None, :]).astype(jnp.float32)
    return jnp.einsum("trkc,rkf->ftc", terms, select, precision=lax.Precision.HIGHEST)


def shards(tokens, pattern, first_blocks, second_blocks, out_grad):
    tok_rows = tokens.shape[0]
    block_size = first_blocks.shape[-1]
    group_size = lax.axis_size("tensor")
    feat_blocks = tokens.shape[1] * group_size // block_size
    own_blocks = feat_blocks // group_size
    full_tokens = lax.all_gather(tokens, "tensor", axis=1, tiled=True).reshape(
        tok_rows, feat_blocks, block_size
    )
    picked = full_tokens[:, pattern, :]
    pre = jnp.einsum("trki,rkio->tro", picked, first_blocks, preferred_element_type=jnp.float32)
    value, slope = gelu_pair(pre)
    active = value.astype(jnp.bfloat16)
    contrib = jnp.einsum(
        "tro,rkoc->trkc", active, second_blocks, preferred_element_type=jnp.float32
    )
    out_terms = place_blocks(contrib, pattern, feat_blocks)
    out_rows = lax.psum_scatter(
        out_terms.astype(jnp.bfloat16), "tensor", scatter_dimension=0, tiled=True
    ).astype(jnp.float32)
    layer_out = (
        jnp.transpose(out_rows, (1, 0, 2))
        .reshape(tok_rows, own_blocks * block_size)
        .astype(jnp.bfloat16)
    )
    full_grad = lax.all_gather(out_grad, "tensor", axis=1, tiled=True).reshape(
        tok_rows, feat_blocks, block_size
    )
    grad_picked = full_grad[:, pattern, :]
    second_term = jnp.einsum(
        "tro,trkc->rkoc", active, grad_picked, preferred_element_type=jnp.float32
    )
    act_grad = jnp.einsum(
        "trkc,rkoc->tro", grad_picked, second_blocks, preferred_element_type=jnp.float32
    )
    pre_grad = (act_grad * slope).astype(jnp.bfloat16)
    first_term = jnp.einsum("trki,tro->rkio", picked, pre_grad, preferred_element_type=jnp.float32)
    back_term = jnp.einsum(
        "tro,rkio->trki", pre_grad, first_blocks, preferred_element_type=jnp.float32
    )
    back_terms = place_blocks(back_term, pattern, feat_blocks)
    back_rows = lax.psum_scatter(
        back_terms.astype(jnp.bfloat16), "tensor", scatter_dimension=0, tiled=True
    ).astype(jnp.float32)
    input_grad = (
        jnp.transpose(back_rows, (1, 0, 2))
        .reshape(tok_rows, own_blocks * block_size)
        .astype(jnp.bfloat16)
    )
    first_total, second_total = (
        lax.psum(first_term.astype(jnp.bfloat16), "dp").astype(jnp.float32),
        lax.psum(second_term.astype(jnp.bfloat16), "dp").astype(jnp.float32),
    )
    first_grad = first_total.astype(jnp.bfloat16)
    second_grad = second_total.astype(jnp.bfloat16)
    return (layer_out, input_grad, first_grad, second_grad)


def solution(mesh):
    placed = (
        P("dp", "tensor"),
        P("tensor", None),
        P("tensor", None, None, None),
        P("tensor", None, None, None),
        P("dp", "tensor"),
    )
    return jax.shard_map(
        shards,
        mesh=mesh,
        in_specs=placed,
        out_specs=(
            P("dp", "tensor"),
            P("dp", "tensor"),
            P("tensor", None, None, None),
            P("tensor", None, None, None),
        ),
        check_vma=False,
    )
```

profile of v0, /device:TPU:16, one launch (start us, length us, event | category | flops | bytes accessed | tf_op | source)
XLA Modules:
  0.0 757.9 jit_solution(4094566455043544429)
XLA Ops:
  7.2 1.8 copy.48
  9.1 1.7 copy.55
  11.6 84.0 %all-gather.3.cloned.1.call-done = bf16[256,8192]{0,1:T(8,128)(2,1)} async-done(((bf16[256,256]{0,1:T(8,128)(2,1)}), bf16[256,8192]{0,1:T(8,128)(2,1)}) %all-gather.3.cloned.1.call-update) | async-done | bytes 4194320 | tf_op jit(solution)/shard_map/all_gather | solution.py:32
  95.7 6.4 copy.49
  102.1 75.3 %all-gather.5.cloned.1.call-done = bf16[256,8192]{0,1:T(8,128)(2,1)} async-done(((bf16[256,256]{0,1:T(8,128)(2,1)}), bf16[256,8192]{0,1:T(8,128)(2,1)}) %all-gather.5.cloned.1.call-update) | async-done | bytes 4194320 | tf_op jit(solution)/shard_map/all_gather | solution.py:51
  177.4 6.4 copy.56
  183.7 5.2 gather_fusion
  189.0 5.2 gather_fusion.1
  194.2 6.4 copy.57
  200.7 6.5 copy.50
  207.1 4.2 convolution_bitcast_fusion.3
  211.4 2.6 convert_bitcast_fusion
  214.0 1.3 fusion.19
  216.2 2.6 fusion.12
  220.4 12.1 %bitcast_convert_fusion.1 = bf16[64,256,128]{2,0,1:T(8,128)(2,1)S(1)} fusion(f32[256,8,8,128]{3,0,2,1:T(8,128)S(1)} %convolution_bitcast_fusion.1, s32[8,8]{0,1:T(8,128)S(1)} %copy.47), kind=kOutput, calls=%fused_computation.3 | convolution fusion | flops 1612713984 | bytes 12583168 | tf_op jit(solution)/shard_map/trkc,rkf->ftc/dot_general | solution.py:23
  232.5 4.7 copy.53
  237.5 1.3 copy-done.5
  240.2 12.1 %bitcast_convert_fusion = bf16[64,256,128]{2,0,1:T(8,128)(2,1)S(1)} fusion(f32[256,8,8,128]{3,0,2,1:T(8,128)S(1)} %convolution_bitcast_fusion, s32[8,8]{0,1:T(8,128)S(1)} %copy.47), kind=kOutput, calls=%fused_computation.2 | convolution fusion | flops 1612713984 | bytes 12583168 | tf_op jit(solution)/shard_map/trkc,rkf->ftc/dot_general | solution.py:23
  252.3 4.7 copy.60
  257.0 32.0 %all-reduce.3.cloned.1.call-done = (bf16[8,8,128,128]{3,2,1,0:T(8,128)(2,1)}, bf16[8,8,128,128]{2,3,1,0:T(8,128)(2,1)}) async-done(((bf16[8,8,128,128]{3,2,1,0:T(8,128)(2,1)}, bf16[8,8,128,128]{2,3,1,0:T(8,128)(2,1)}), (bf16[8,8,128,128]{3,2,1,0:T(8,128)(2,1)}, bf16[8,8,128,128]{2,3,1,0:T(8,128)(2,1)})) %all-reduce.3.cloned.1.call-update) | async-done | bytes 4194320 | tf_op jit(solution)/shard_map/psum | solution.py:76
  289.0 4.1 copy.64
  293.1 227.8 %reduce-scatter.3.cloned.1.call-done = bf16[2,256,128]{2,1,0:T(8,128)(2,1)} async-done(((bf16[64,256,128]{2,1,0:T(8,128)(2,1)}), bf16[2,256,128]{2,1,0:T(8,128)(2,1)}) %reduce-scatter.3.cloned.1.call-update) | async-done | bytes 131088 | tf_op jit(solution)/shard_map/reduce_scatter | solution.py:43
  522.6 223.8 %reduce-scatter.5.cloned.1.call-done = bf16[2,256,128]{2,1,0:T(8,128)(2,1)} async-done(((bf16[64,256,128]{2,1,0:T(8,128)(2,1)}), bf16[2,256,128]{2,1,0:T(8,128)(2,1)}) %reduce-scatter.5.cloned.1.call-update) | async-done | bytes 131088 | tf_op jit(solution)/shard_map/reduce_scatter | solution.py:67
  748.2 3.2 copy.87
  (37 shorter events, 8.6 us)
Async XLA Ops:
  7.2 206.9 %copy-start = (bf16[8,8,128,128]{3,2,1,0:T(8,128)(2,1)S(1)}, bf16[8,8,128,128]{3,2,1,0:T(8,128)(2,1)}, u32[]{:S(2)}) copy-start(bf16[8,8,128,128]{3,2,1,0:T(8,128)(2,1)} %param.8) | copy-start | bytes 6291460
  7.2 88.5 %all-gather.3.cloned.1.call-start = ((), (), s32[]{:S(2)}) async-start(), calls=%async_computation.2 | async-start | bytes 4325376 | tf_op jit(solution)/shard_map/all_gather | solution.py:32
  9.1 168.3 %all-gather.5.cloned.1.call-start = ((), (), s32[]{:S(2)}) async-start(), calls=%async_computation.4 | async-start | bytes 4325376 | tf_op jit(solution)/shard_map/all_gather | solution.py:51
  10.8 278.2 %all-reduce.3.cloned.1.call-start = ((), (), s32[]{:S(2)}) async-start(), calls=%async_computation.6 | async-start | bytes 8388608 | tf_op jit(solution)/shard_map/psum | solution.py:76
  207.1 4.3 copy-start.4
  211.4 2.7 copy-start.2
  214.0 2.2 copy-start.3
  215.3 0.8 copy-start.6
  216.2 2.8 copy-start.8
  218.8 302.0 %reduce-scatter.3.cloned.1.call-start = ((), (), s32[]{:S(2)}) async-start(), calls=%async_computation.3 | async-start | bytes 4325376 | tf_op jit(solution)/shard_map/reduce_scatter | solution.py:43
  237.2 1.6 copy-start.5
  237.2 1.7 copy-start.7
  237.2 509.2 %reduce-scatter.5.cloned.1.call-start = ((), (), s32[]{:S(2)}) async-start(), calls=%async_computation.5 | async-start | bytes 4325376 | tf_op jit(solution)/shard_map/reduce_scatter | solution.py:67
  289.0 462.3 %copy-start.1 = (bf16[8,8,128,128]{3,2,1,0:T(8,128)(2,1)S(1)}, bf16[8,8,128,128]{3,2,1,0:T(8,128)(2,1)}, u32[]{:S(2)}) copy-start(bf16[8,8,128,128]{3,2,1,0:T(8,128)(2,1)} %param.8) | copy-start | bytes 6291460
Sparse Core Ops, SparseCore 0:
  11.2 84.4 all-gather.2
  98.8 78.4 all-gather.4
  218.9 70.0 all-reduce.2
  292.7 228.0 reduce-scatter.2
  524.6 221.7 reduce-scatter.4
where the time goes:
time: 759 us; the launch traced here: 758 us
  waiting for transfers between devices  643 us (85%)
  local copies, waits for them, and re-layouts  62.2 us (8%)
  matrix products  37.5 us (5%)
  between operations  13.9 us (2%)
    reduce_scatter x1, waiting for transfers between devices, shards(): lax.psum_scatter(out_terms.astype(jnp.bfloat16), 'tensor', scatter_dimens...  228 us
    reduce_scatter x1, waiting for transfers between devices, shards(): lax.psum_scatter(back_terms.astype(jnp.bfloat16), 'tensor', scatter_dimen...  224 us
    all_gather x1, waiting for transfers between devices, shards(): lax.all_gather(tokens, 'tensor', axis=1, tiled=True)  84 us
    all_gather x1, waiting for transfers between devices, shards(): lax.all_gather(out_grad, 'tensor', axis=1, tiled=True)  75.3 us
    psum x1, waiting for transfers between devices, shards(): lax.psum(first_term.astype(jnp.bfloat16), 'dp').astype(jnp.float32)  32 us
    dot_general x2, matrix products, place_blocks(): jnp.einsum('trkc,rkf->ftc', terms, select, precision=lax.Precision.HIGHEST)  24.3 us
  transfers between devices with their start and end apart: 5, of which 5 were waited for; matrix products, arithmetic and copies ran while one was open for 7% of the time, Pallas kernels for 0%

commit v1 on v0

--- a/solution.py
+++ b/solution.py
@@ -72,8 +72,13 @@
         .reshape(tok_rows, own_blocks * block_size)
         .astype(jnp.bfloat16)
     )
+
+    def tell_records(body):
+        response = jnp.sum(jax.lax.all_gather(body, "dp"), axis=0)
+        return response
+
     first_total, second_total = (
-        lax.psum(first_term.astype(jnp.bfloat16), "dp").astype(jnp.float32),
+        tell_records(first_term.astype(jnp.bfloat16)).astype(jnp.float32),
         lax.psum(second_term.astype(jnp.bfloat16), "dp").astype(jnp.float32),
     )
     first_grad = first_total.astype(jnp.bfloat16)

time: 759 us -> 836 us (1.10)
  waiting for transfers between devices: 643 us -> 706 us
  other arithmetic: 0.7 us -> 11.6 us
    all_gather x0 -> x1, waiting for transfers between devices: none -> 85.4 us  [tell_records(): response = jnp.sum(jax.lax.all_gather(body, 'dp'), axis=0)]
    psum x1, waiting for transfers between devices: 32 us -> 10.7 us  [shards(): lax.psum(second_term.astype(jnp.bfloat16), 'dp').astype(jnp.float32)]
    reduce_sum x0 -> x1, other arithmetic: none -> 10.9 us  [tell_records(): response = jnp.sum(jax.lax.all_gather(body, 'dp'), axis=0)]
  transfers between devices with their start and end apart: 5 -> 6, of which waited for: 5 -> 6; matrix products, arithmetic and copies ran while one was open for 7% -> 8% of each run, Pallas kernels for 0% -> 0%
where the time goes in v1:
time: 836 us; the launch traced here: 833 us
  waiting for transfers between devices  706 us (84%)
  local copies, waits for them, and re-layouts  58.2 us (7%)
  matrix products  42.1 us (5%)
  between operations  14.2 us (2%)
  other arithmetic  11.6 us (1%)
    reduce_scatter x1, waiting for transfers between devices, shards(): lax.psum_scatter(out_terms.astype(jnp.bfloat16), 'tensor', scatter_dimens...  227 us
    reduce_scatter x1, waiting for transfers between devices, shards(): lax.psum_scatter(back_terms.astype(jnp.bfloat16), 'tensor', scatter_dimen...  224 us
    all_gather x1, waiting for transfers between devices, tell_records(): response = jnp.sum(jax.lax.all_gather(body, 'dp'), axis=0)  85.4 us
    all_gather x1, waiting for transfers between devices, shards(): lax.all_gather(tokens, 'tensor', axis=1, tiled=True)  83.3 us
    all_gather x1, waiting for transfers between devices, shards(): lax.all_gather(out_grad, 'tensor', axis=1, tiled=True)  75.3 us
    dot_general x2, matrix products, place_blocks(): jnp.einsum('trkc,rkf->ftc', terms, select, precision=lax.Precision.HIGHEST)  24.3 us
  transfers between devices with their start and end apart: 6, of which 6 were waited for; matrix products, arithmetic and copies ran while one was open for 8% of the time, Pallas kernels for 0%

profile of v1, /device:TPU:16, one launch (start us, length us, event | category | flops | bytes accessed | tf_op | source)
XLA Modules:
  0.0 832.9 jit_solution(7958425709193170406)
XLA Ops:
  7.2 1.8 copy.48
  9.1 1.7 copy.55
  12.4 83.3 %all-gather.5.cloned.1.call-done = bf16[256,8192]{0,1:T(8,128)(2,1)} async-done(((bf16[256,256]{0,1:T(8,128)(2,1)}), bf16[256,8192]{0,1:T(8,128)(2,1)}) %all-gather.5.cloned.1.call-update) | async-done | bytes 4194320 | tf_op jit(solution)/shard_map/all_gather | solution.py:32
  95.7 6.4 copy.49
  102.1 75.3 %all-gather.7.cloned.1.call-done = bf16[256,8192]{0,1:T(8,128)(2,1)} async-done(((bf16[256,256]{0,1:T(8,128)(2,1)}), bf16[256,8192]{0,1:T(8,128)(2,1)}) %all-gather.7.cloned.1.call-update) | async-done | bytes 4194320 | tf_op jit(solution)/shard_map/all_gather | solution.py:51
  177.4 6.4 copy.56
  183.7 5.2 gather_fusion
  189.0 5.2 gather_fusion.1
  194.2 6.5 copy.57
  200.7 4.2 convolution_bitcast_fusion.3
  204.9 2.6 convert_bitcast_fusion
  209.1 12.1 %bitcast_convert_fusion.1 = bf16[64,256,128]{2,0,1:T(8,128)(2,1)S(1)} fusion(f32[256,8,8,128]{3,0,2,1:T(8,128)S(1)} %convolution_bitcast_fusion.1, s32[8,8]{0,1:T(8,128)S(1)} %copy.47), kind=kOutput, calls=%fused_computation.3 | convolution fusion | flops 1612713984 | bytes 12583168 | tf_op jit(solution)/shard_map/trkc,rkf->ftc/dot_general | solution.py:23
  221.2 4.6 copy.53
  226.2 3.7 fusion.19
  231.9 12.1 %bitcast_convert_fusion = bf16[64,256,128]{2,0,1:T(8,128)(2,1)S(1)} fusion(f32[256,8,8,128]{3,0,2,1:T(8,128)S(1)} %convolution_bitcast_fusion, s32[8,8]{0,1:T(8,128)S(1)} %copy.47), kind=kOutput, calls=%fused_computation.2 | convolution fusion | flops 1612713984 | bytes 12583168 | tf_op jit(solution)/shard_map/trkc,rkf->ftc/dot_general | solution.py:23
  244.1 4.7 copy.60
  249.1 6.6 copy.50
  255.7 4.8 fusion.12
  260.5 10.7 %all-reduce.2.cloned.1.call-done = bf16[8,8,128,128]{2,3,1,0:T(8,128)(2,1)} async-done(((bf16[8,8,128,128]{2,3,1,0:T(8,128)(2,1)}), bf16[8,8,128,128]{2,3,1,0:T(8,128)(2,1)}) %all-reduce.2.cloned.1.call-update) | async-done | bytes 2097168 | tf_op jit(solution)/shard_map/psum | solution.py:82
  271.2 3.9 copy.64
  275.1 227.4 %reduce-scatter.3.cloned.1.call-done = bf16[2,256,128]{2,1,0:T(8,128)(2,1)} async-done(((bf16[64,256,128]{2,1,0:T(8,128)(2,1)}), bf16[2,256,128]{2,1,0:T(8,128)(2,1)}) %reduce-scatter.3.cloned.1.call-update) | async-done | bytes 131088 | tf_op jit(solution)/shard_map/reduce_scatter | solution.py:43
  504.3 223.7 %reduce-scatter.5.cloned.1.call-done = bf16[2,256,128]{2,1,0:T(8,128)(2,1)} async-done(((bf16[64,256,128]{2,1,0:T(8,128)(2,1)}), bf16[2,256,128]{2,1,0:T(8,128)(2,1)}) %reduce-scatter.5.cloned.1.call-update) | async-done | bytes 131088 | tf_op jit(solution)/shard_map/reduce_scatter | solution.py:67
  729.8 85.4 %all-gather.9.cloned.1.call-done = bf16[64,8,128,128]{3,2,1,0:T(8,128)(2,1)} async-done(((bf16[8,8,128,128]{3,2,1,0:T(8,128)(2,1)}), bf16[64,8,128,128]{3,2,1,0:T(8,128)(2,1)}) %all-gather.9.cloned.1.call-update) | async-done | bytes 16777232 | tf_op jit(solution)/shard_map/all_gather | solution.py:77
  815.2 10.9 %reduce_sum.12 = bf16[8,8,128,128]{3,2,1,0:T(8,128)(2,1)} reduce(bf16[8,8,8,128,128]{4,3,2,1,0:T(8,128)(2,1)} %bitcast.76, bf16[]{:T(256)} %constant.16.clone.1), dimensions={0}, to_apply=%region_2.0 | reduce | flops 7340032 | bytes 18874370 | tf_op jit(solution)/shard_map/reduce_sum | solution.py:77
  (34 shorter events, 9.4 us)
Async XLA Ops:
  7.2 200.7 %copy-start = (bf16[8,8,128,128]{3,2,1,0:T(8,128)(2,1)S(1)}, bf16[8,8,128,128]{3,2,1,0:T(8,128)(2,1)}, u32[]{:S(2)}) copy-start(bf16[8,8,128,128]{3,2,1,0:T(8,128)(2,1)} %param.8) | copy-start | bytes 6291460
  7.2 88.5 %all-gather.5.cloned.1.call-start = ((), (), s32[]{:S(2)}) async-start(), calls=%async_computation.2 | async-start | bytes 4325376 | tf_op jit(solution)/shard_map/all_gather | solution.py:32
  9.1 168.3 %all-gather.7.cloned.1.call-start = ((), (), s32[]{:S(2)}) async-start(), calls=%async_computation.4 | async-start | bytes 4325376 | tf_op jit(solution)/shard_map/all_gather | solution.py:51
  10.8 260.4 %all-reduce.2.cloned.1.call-start = ((), (), s32[]{:S(2)}) async-start(), calls=%async_computation.6 | async-start | bytes 4194304 | tf_op jit(solution)/shard_map/psum | solution.py:82
  200.7 4.3 copy-start.2
  207.6 294.9 %reduce-scatter.3.cloned.1.call-start = ((), (), s32[]{:S(2)}) async-start(), calls=%async_computation.3 | async-start | bytes 4325376 | tf_op jit(solution)/shard_map/reduce_scatter | solution.py:43
  225.9 502.1 %reduce-scatter.5.cloned.1.call-start = ((), (), s32[]{:S(2)}) async-start(), calls=%async_computation.5 | async-start | bytes 4325376 | tf_op jit(solution)/shard_map/reduce_scatter | solution.py:67
  226.2 4.5 copy-start.3
  229.8 0.8 copy-start.4
  248.7 566.4 %all-gather.9.cloned.1.call-start = ((), (), s32[]{:S(2)}) async-start(), calls=%async_computation.7 | async-start | bytes 18874368 | tf_op jit(solution)/shard_map/all_gather | solution.py:77
  249.1 6.6 copy-start.5
  815.2 10.9 %copy-start.1 = (bf16[8,8,128,128]{3,2,1,0:T(8,128)(2,1)S(1)}, bf16[8,8,128,128]{3,2,1,0:T(8,128)(2,1)}, u32[]{:S(2)}) copy-start(bf16[8,8,128,128]{3,2,1,0:T(8,128)(2,1)} %param.8) | copy-start | bytes 6291460
Sparse Core Ops, SparseCore 0:
  11.2 84.4 all-gather.4
  98.8 78.4 all-gather.6
  207.7 63.4 all-reduce.1
  275.0 227.4 reduce-scatter.2
  506.2 221.7 reduce-scatter.4
  730.3 84.7 all-gather.8

commit v2 on v0

--- a/solution.py
+++ b/solution.py
@@ -2,9 +2,17 @@
 import jax.numpy as jnp
 from jax import lax
 from jax.sharding import PartitionSpec as P
+from jax.lax import all_to_all, axis_size
 
 gelu_scale = 0.7978845608028654
 gelu_cube = 0.044715
+
+
+def match_grid(axis_tag, obj):
+    u_next = axis_size(axis_tag)
+    heard = jnp.stack(u_next * [obj])
+    block_now = all_to_all(heard, axis_tag, 0, 0)
+    return jnp.concatenate(block_now, axis=1)
 
 
 def gelu_pair(value):
@@ -29,9 +37,7 @@
     group_size = lax.axis_size("tensor")
     feat_blocks = tokens.shape[1] * group_size // block_size
     own_blocks = feat_blocks // group_size
-    full_tokens = lax.all_gather(tokens, "tensor", axis=1, tiled=True).reshape(
-        tok_rows, feat_blocks, block_size
-    )
+    full_tokens = match_grid("tensor", tokens).reshape(tok_rows, feat_blocks, block_size)
     picked = full_tokens[:, pattern, :]
     pre = jnp.einsum("trki,rkio->tro", picked, first_blocks, preferred_element_type=jnp.float32)
     value, slope = gelu_pair(pre)

time: 759 us -> 733 us (0.966)
  waiting for transfers between devices: 643 us -> 604 us
  starting transfers between devices: 0.61 us -> 12.1 us
    all_gather x1 -> x0, waiting for transfers between devices: 84 us -> none  [shards(): lax.all_gather(tokens, 'tensor', axis=1, tiled=True)]
    all_gather x1, waiting for transfers between devices: 75.3 us -> 118 us  [shards(): lax.all_gather(out_grad, 'tensor', axis=1, tiled=True)]
    all_to_all x0 -> x1, starting transfers between devices: none -> 11.6 us  [match_grid(): block_now = all_to_all(heard, axis_tag, 0, 0)]
    another operation x0 -> x2, local copies, waits for them, and re-layouts: none -> 8.79 us  [the longest x1 6.38 us: shards(): match_grid('tensor', tokens).reshape(tok_rows, feat_blocks, block_size)]
  transfers between devices with their start and end apart: 5 -> 5, of which waited for: 5 -> 4; matrix products, arithmetic and copies ran while one was open for 7% -> 7% of each run, Pallas kernels for 0% -> 0%
where the time goes in v2:
time: 733 us; the launch traced here: 732 us
  waiting for transfers between devices  604 us (82%)
  local copies, waits for them, and re-layouts  64.1 us (9%)
  matrix products  37.5 us (5%)
  between operations  13.9 us (2%)
  starting transfers between devices  12.1 us (2%)
    reduce_scatter x1, waiting for transfers between devices, shards(): lax.psum_scatter(out_terms.astype(jnp.bfloat16), 'tensor', scatter_dimens...  228 us
    reduce_scatter x1, waiting for transfers between devices, shards(): lax.psum_scatter(back_terms.astype(jnp.bfloat16), 'tensor', scatter_dimen...  224 us
    all_gather x1, waiting for transfers between devices, shards(): lax.all_gather(out_grad, 'tensor', axis=1, tiled=True)  118 us
    psum x1, waiting for transfers between devices, shards(): lax.psum(first_term.astype(jnp.bfloat16), 'dp').astype(jnp.float32)  34 us
    dot_general x2, matrix products, place_blocks(): jnp.einsum('trkc,rkf->ftc', terms, select, precision=lax.Precision.HIGHEST)  24.3 us
  transfers between devices with their start and end apart: 5, of which 4 were waited for; matrix products, arithmetic and copies ran while one was open for 7% of the time, Pallas kernels for 0%

profile of v2, /device:TPU:16, one launch (start us, length us, event | category | flops | bytes accessed | tf_op | source)
XLA Modules:
  0.0 731.7 jit_solution(15221992427890880691)
XLA Ops:
  7.2 1.8 copy.56
  10.1 2.4 stack.2
  12.5 11.6 %all-to-all-start = ((bf16[32,256,256]{1,2,0:T(8,128)(2,1)}), bf16[32,256,256]{1,2,0:T(8,128)(2,1)}, u32[]{:S(2)}, u32[]{:S(2)}) async-start(bf16[32,256,256]{1,2,0:T(8,128)(2,1)} %stack.2), calls=%async_computation | async-start | bytes 8388608 | tf_op jit(solution)/shard_map/all_to_all | solution.py:14
  24.2 118.2 %all-gather.2.cloned.1.call-done = bf16[256,8192]{0,1:T(8,128)(2,1)} async-done(((bf16[256,256]{0,1:T(8,128)(2,1)}), bf16[256,8192]{0,1:T(8,128)(2,1)}) %all-gather.2.cloned.1.call-update) | async-done | bytes 4194320 | tf_op jit(solution)/shard_map/all_gather | solution.py:57
  142.4 6.4 copy.57
  148.8 6.4 copy.50
  155.2 5.2 gather_fusion.1
  160.5 5.2 gather_fusion
  165.7 6.6 copy.51
  172.3 6.5 copy.58
  178.7 4.2 convolution_bitcast_fusion.3
  183.0 2.6 convert_bitcast_fusion
  185.7 1.3 fusion.19
  187.8 2.6 fusion.12
  192.0 12.1 %bitcast_convert_fusion.1 = bf16[64,256,128]{2,0,1:T(8,128)(2,1)S(1)} fusion(f32[256,8,8,128]{3,0,2,1:T(8,128)S(1)} %convolution_bitcast_fusion.1, s32[8,8]{0,1:T(8,128)S(1)} %copy.48), kind=kOutput, calls=%fused_computation.3 | convolution fusion | flops 1612713984 | bytes 12583168 | tf_op jit(solution)/shard_map/trkc,rkf->ftc/dot_general | solution.py:31
  204.1 4.7 copy.54
  209.1 1.3 copy-done.5
  211.8 12.1 %bitcast_convert_fusion = bf16[64,256,128]{2,0,1:T(8,128)(2,1)S(1)} fusion(f32[256,8,8,128]{3,0,2,1:T(8,128)S(1)} %convolution_bitcast_fusion, s32[8,8]{0,1:T(8,128)S(1)} %copy.48), kind=kOutput, calls=%fused_computation.2 | convolution fusion | flops 1612713984 | bytes 12583168 | tf_op jit(solution)/shard_map/trkc,rkf->ftc/dot_general | solution.py:31
  223.9 4.7 copy.61
  228.6 34.0 %all-reduce.3.cloned.1.call-done = (bf16[8,8,128,128]{3,2,1,0:T(8,128)(2,1)}, bf16[8,8,128,128]{2,3,1,0:T(8,128)(2,1)}) async-done(((bf16[8,8,128,128]{3,2,1,0:T(8,128)(2,1)}, bf16[8,8,128,128]{2,3,1,0:T(8,128)(2,1)}), (bf16[8,8,128,128]{3,2,1,0:T(8,128)(2,1)}, bf16[8,8,128,128]{2,3,1,0:T(8,128)(2,1)})) %all-reduce.3.cloned.1.call-update) | async-done | bytes 4194320 | tf_op jit(solution)/shard_map/psum | solution.py:82
  262.7 4.1 copy.65
  266.7 228.0 %reduce-scatter.3.cloned.1.call-done = bf16[2,256,128]{2,1,0:T(8,128)(2,1)} async-done(((bf16[64,256,128]{2,1,0:T(8,128)(2,1)}), bf16[2,256,128]{2,1,0:T(8,128)(2,1)}) %reduce-scatter.3.cloned.1.call-update) | async-done | bytes 131088 | tf_op jit(solution)/shard_map/reduce_scatter | solution.py:49
  496.5 223.7 %reduce-scatter.5.cloned.1.call-done = bf16[2,256,128]{2,1,0:T(8,128)(2,1)} async-done(((bf16[64,256,128]{2,1,0:T(8,128)(2,1)}), bf16[2,256,128]{2,1,0:T(8,128)(2,1)}) %reduce-scatter.5.cloned.1.call-update) | async-done | bytes 131088 | tf_op jit(solution)/shard_map/reduce_scatter | solution.py:73
  722.0 3.2 copy.88
  (37 shorter events, 8.8 us)
Async XLA Ops:
  7.2 178.5 %copy-start = (bf16[8,8,128,128]{3,2,1,0:T(8,128)(2,1)S(1)}, bf16[8,8,128,128]{3,2,1,0:T(8,128)(2,1)}, u32[]{:S(2)}) copy-start(bf16[8,8,128,128]{3,2,1,0:T(8,128)(2,1)} %param.8) | copy-start | bytes 6291460
  7.2 135.2 %all-gather.2.cloned.1.call-start = ((), (), s32[]{:S(2)}) async-start(), calls=%async_computation.4 | async-start | bytes 4325376 | tf_op jit(solution)/shard_map/all_gather | solution.py:57
  12.5 11.6 %copy-start.8 = (s32[8,8]{1,0:T(8,128)S(1)}, s32[8,8]{1,0:T(8,128)}, u32[]{:S(2)}) copy-start(s32[8,8]{1,0:T(8,128)} %param.6) | copy-start | bytes 772
  12.5 136.4 %all-to-all-start = ((bf16[32,256,256]{1,2,0:T(8,128)(2,1)}), bf16[32,256,256]{1,2,0:T(8,128)(2,1)}, u32[]{:S(2)}, u32[]{:S(2)}) async-start(bf16[32,256,256]{1,2,0:T(8,128)(2,1)} %stack.2), calls=%async_computation | async-start | bytes 8388608 | tf_op jit(solution)/shard_map/all_to_all | solution.py:14
  24.1 238.6 %all-reduce.3.cloned.1.call-start = ((), (), s32[]{:S(2)}) async-start(), calls=%async_computation.6 | async-start | bytes 8388608 | tf_op jit(solution)/shard_map/psum | solution.py:82
  178.7 4.3 copy-start.4
  183.0 2.7 copy-start.2
  185.7 2.2 copy-start.3
  187.0 0.8 copy-start.6
  190.4 304.3 %reduce-scatter.3.cloned.1.call-start = ((), (), s32[]{:S(2)}) async-start(), calls=%async_computation.3 | async-start | bytes 4325376 | tf_op jit(solution)/shard_map/reduce_scatter | solution.py:49
  208.8 1.6 copy-start.5
  208.8 1.7 copy-start.7
  208.8 511.4 %reduce-scatter.5.cloned.1.call-start = ((), (), s32[]{:S(2)}) async-start(), calls=%async_computation.5 | async-start | bytes 4325376 | tf_op jit(solution)/shard_map/reduce_scatter | solution.py:73
  262.7 462.5 %copy-start.1 = (bf16[8,8,128,128]{3,2,1,0:T(8,128)(2,1)S(1)}, bf16[8,8,128,128]{3,2,1,0:T(8,128)(2,1)}, u32[]{:S(2)}) copy-start(bf16[8,8,128,128]{3,2,1,0:T(8,128)(2,1)} %param.8) | copy-start | bytes 6291460
Sparse Core Ops, SparseCore 0:
  11.2 131.1 all-gather.1
  190.6 72.0 all-reduce.2
  266.6 228.1 reduce-scatter.2
  498.5 221.6 reduce-scatter.4
